TPU v7x, 32 devices: a whole 2x2x4 slice. The times are simulated.
32 devices in a mesh: row: 4 (over z), col: 8 (over y, x, core).
Axes of the slice: x: 2, y: 2, z: 4, core: 2. Of those that a mesh axis runs over, the one named last changes fastest.
Arguments:
- src_points: bfloat16 [512, 32, 256], P('row'), may hold values from -6 to 6
- tgt_points: bfloat16 [64, 32, 256], P('col'), may hold values from -6 to 6
- log_src: float32 [512, 256], P('row'), may hold values from -4 to 4
- log_tgt: float32 [64, 256], P('col'), may hold values from -4 to 4
- tgt_potential: float32 [64, 256], P('col'), may hold values from -1 to 25
- pattern: int32 [512, 4], P('row'), may hold values from 0 to 63, as said below
Outputs:
- src_new: float32 [512, 256], P('row')
- tgt_new: float32 [64, 256], P('col')
Inputs may be any that keep to these rules, and one draw needn't show every extreme that they name: `pattern`: each row names 4 different target blocks. For every index of row and every index of col, at most 128 of the entries in that index's source blocks name a target block held by that index of col, and exactly 128 do for some index of col. Every target block is named by some entry.
All inputs are finite; a program needn't handle non-finite values.
Results may differ from a plain program's by a relative error of at most 0.0015.
Values may be sent and summed in bfloat16 or wider, within the bound.
No kernel may reach another device: no remote copies, remote signals or barrier semaphores. Data moves between devices by JAX's collectives and lax.ppermute only.
A program may use at most 64 MiB of HBM per device.

v0:
```python
import math

import jax
import jax.numpy as jnp
from jax import lax
from jax.sharding import PartitionSpec as P

DIM = 32
FANOUT = 4
PAIR_MEAN = 64


epsilon = 0.1
very_low = -1e30
entry_batch = 8


def joined(value, axis, join):
    pieces = jax.tree.map(lambda part: lax.all_gather(part, axis), value)
    head = jax.tree.map(lambda part: part[0], pieces)
    tail = jax.tree.map(lambda part: part[1:], pieces)
    subtotal, _ = lax.scan(lambda subtotal, share: (join(subtotal, share), None), head, tail)
    return subtotal


def merge_parts(left_part, right_part):
    top_score = jnp.maximum(left_part[0], right_part[0])
    exp_total = left_part[1] * jnp.exp(left_part[0] - top_score) + right_part[1] * jnp.exp(
        right_part[0] - top_score
    )
    return (top_score, exp_total)


def pick_rows(table, row_ids, precise):
    table_rows = table.shape[0]
    flat = table.reshape(table_rows, -1)
    selector = (row_ids[:, None] == jnp.arange(table_rows, dtype=jnp.int32)[None, :]).astype(
        flat.dtype
    )
    if precise:
        picked = jnp.dot(
            selector, flat, precision=lax.Precision.HIGHEST, preferred_element_type=jnp.float32
        )
    else:
        picked = jnp.dot(selector, flat, preferred_element_type=jnp.float32).astype(table.dtype)
    return picked.reshape((row_ids.shape[0],) + table.shape[1:])


def collect_rows(row_total_count, row_ids, part_top, part_total):
    group = math.gcd(row_total_count, 32)

    def group_top(first_row):
        group_ids = first_row + jnp.arange(group, dtype=jnp.int32)
        member = row_ids[None, :] == group_ids[:, None]
        return jnp.max(jnp.where(member[:, :, None], part_top[None, :, :], very_low), axis=1)

    starts = jnp.arange(0, row_total_count, group, dtype=jnp.int32)
    block_top = lax.map(group_top, starts).reshape(row_total_count, part_top.shape[1])
    picked_top = pick_rows(block_top, row_ids, True)
    member_all = (row_ids[None, :] == jnp.arange(row_total_count, dtype=jnp.int32)[:, None]).astype(
        jnp.float32
    )
    block_total = jnp.dot(
        member_all,
        part_total * jnp.exp(part_top - picked_top),
        precision=lax.Precision.HIGHEST,
        preferred_element_type=jnp.float32,
    )
    return (block_top, block_total)


def on_device(src_points, tgt_points, log_src, log_tgt, tgt_potential, pattern):
    cell_count = src_points.shape[2]
    col_index = lax.axis_index("col")
    flat_targets = pattern.reshape(-1)
    all_points = lax.all_gather(tgt_points, "col", axis=0, tiled=True)
    all_potential = lax.all_gather(tgt_potential, "col", axis=0, tiled=True)
    slot_count = PAIR_MEAN
    chosen = col_index * slot_count + jnp.arange(slot_count, dtype=jnp.int32)
    slot_src = chosen // FANOUT
    slot_tgt = lax.dynamic_slice_in_dim(flat_targets, col_index * slot_count, slot_count, 0)
    in_use = jnp.ones((slot_count,), jnp.bool_)
    turn_count = slot_count // entry_batch
    slot_src_points = pick_rows(src_points, slot_src, False)
    slot_tgt_points = pick_rows(all_points, slot_tgt, False)
    slot_potential = pick_rows(all_potential, slot_tgt, True)
    point_shape = (turn_count, entry_batch) + src_points.shape[1:]
    batches = (
        slot_src_points.reshape(point_shape),
        slot_tgt_points.reshape(point_shape),
        in_use.reshape(turn_count, entry_batch),
    )

    def distances(src_block, tgt_block):
        products = jnp.einsum(
            "gdi,gdj->gij", src_block, tgt_block, preferred_element_type=jnp.float32
        )
        src_square = jnp.sum(jnp.square(src_block.astype(jnp.float32)), axis=1)
        tgt_square = jnp.sum(jnp.square(tgt_block.astype(jnp.float32)), axis=1)
        return (src_square[:, :, None] + tgt_square[:, None, :] - 2.0 * products) / DIM

    def row_terms(costs, potential_rows, used):
        scores = (potential_rows[:, None, :] - costs) / epsilon
        top_score = jnp.max(scores, axis=2)
        exp_total = jnp.sum(jnp.exp(scores - top_score[:, :, None]), axis=2)
        top_score = jnp.where(used[:, None], top_score, very_low)
        exp_total = jnp.where(used[:, None], exp_total, 0.0)
        return (top_score, exp_total)

    row_batches = batches + (slot_potential.reshape(turn_count, entry_batch, cell_count),)

    def row_fresh(state_in, members):
        return (state_in, row_terms(distances(members[0], members[1]), members[3], members[2]))

    row_out = lax.scan(row_fresh, None, row_batches)[1]
    row_top = row_out[0].reshape(slot_count, cell_count)
    row_total = row_out[1].reshape(slot_count, cell_count)
    own_count = slot_count // FANOUT
    own_start = col_index * own_count
    own_top = jnp.max(row_top.reshape(own_count, FANOUT, cell_count), axis=1)
    own_total = jnp.sum(
        (row_total * jnp.exp(row_top - jnp.repeat(own_top, FANOUT, axis=0))).reshape(
            own_count, FANOUT, cell_count
        ),
        axis=1,
    )
    own_log = lax.dynamic_slice_in_dim(log_src, own_start, own_count, 0)
    own_new = epsilon * own_log - epsilon * (own_top + jnp.log(own_total))
    src_new = lax.all_gather(own_new, "col", axis=0, tiled=True)
    slot_src_new = pick_rows(src_new, slot_src, True).reshape(turn_count, entry_batch, cell_count)

    def column_terms(costs, src_rows, used):
        weights = (src_rows[:, :, None] - costs) / epsilon
        top_score = jnp.max(weights, axis=1)
        exp_total = jnp.sum(jnp.exp(weights - top_score[:, None, :]), axis=1)
        top_score = jnp.where(used[:, None], top_score, very_low)
        exp_total = jnp.where(used[:, None], exp_total, 0.0)
        return (top_score, exp_total)

    def column_fresh(state_in, members):
        return (state_in, column_terms(distances(members[0], members[1]), members[3], members[2]))

    column_out = lax.scan(column_fresh, None, batches + (slot_src_new,))[1]
    column_top = column_out[0].reshape(slot_count, cell_count)
    column_total = column_out[1].reshape(slot_count, cell_count)
    tgt_rows = all_points.shape[0]
    target_top, target_total = collect_rows(tgt_rows, slot_tgt, column_top, column_total)
    sent_top, sent_total = (
        lax.all_to_all(target_top[:, None, :], "col", split_axis=0, concat_axis=1, tiled=True),
        lax.all_to_all(target_total[:, None, :], "col", split_axis=0, concat_axis=1, tiled=True),
    )
    local_top = jnp.max(sent_top, axis=1)
    local_total = jnp.sum(sent_total * jnp.exp(sent_top - local_top[:, None, :]), axis=1)
    final_top, final_total = joined((local_top, local_total), "row", merge_parts)
    tgt_new = epsilon * log_tgt - epsilon * (final_top + jnp.log(final_total))
    return (src_new, tgt_new)


def solution(mesh):
    placed = (
        P("row", None, None),
        P("col", None, None),
        P("row", None),
        P("col", None),
        P("col", None),
        P("row", None),
    )
    return jax.shard_map(
        on_device,
        mesh=mesh,
        in_specs=placed,
        out_specs=(P("row", None), P("col", None)),
        check_vma=False,
    )
```

profile of v0, /device:TPU:0, one launch (start us, length us, event | category | flops | bytes accessed | tf_op | source)
XLA Modules:
  0.0 134.5 jit_solution(16808524770713753963)
XLA Ops:
  7.9 0.8 copy.24
  8.8 3.0 %copy.32 = bf16[16,8,32,256]{3,1,2,0:T(8,128)(2,1)S(1)} copy(bf16[16,8,32,256]{3,2,1,0:T(8,128)(2,1)} %bitcast.132) | data formatting | bytes 4194304
  12.7 10.7 %all_gather.21 = f32[64,256]{1,0:T(8,128)S(1)} all-gather(f32[8,256]{1,0:T(8,128)S(1)} %copy-done), channel_id=1, replica_groups=mesh['row'=4,'col'=8] {'col'}, dimensions={0}, use_global_device_ids=true | all-gather | bytes 73728 | tf_op jit(solution)/shard_map/all_gather | solution.py:77
  23.6 12.4 %all-gather.4.cloned.1.call-done = bf16[64,32,256]{2,1,0:T(8,128)(2,1)} async-done(((bf16[8,32,256]{2,1,0:T(8,128)(2,1)}), bf16[64,32,256]{2,1,0:T(8,128)(2,1)}) %all-gather.4.cloned.1.call-update) | async-done | bytes 1048592 | tf_op jit(solution)/shard_map/all_gather | solution.py:76
  36.0 1.9 %copy.33 = bf16[8,8,32,256]{3,1,2,0:T(8,128)(2,1)S(1)} copy(bf16[8,8,32,256]{3,2,1,0:T(8,128)(2,1)} %bitcast.133) | data formatting | bytes 2097152
  38.7 14.9 %while.46 = (s32[]{:T(128)}, f32[8,8,256]{2,1,0:T(8,128)S(1)}, f32[8,8,256]{2,1,0:T(8,128)S(1)}, f32[8,8,256]{2,1,0:T(8,128)S(1)}, bf16[8,8,32,256]{3,2,1,0:T(8,...) while((s32[]{:T(128)}, f32[8,8,256]{2,1,0:T(8,128)S(1)}, f32[8,8,256]{2,1,0:T(8,128)S(1)}, ...), condition=%wide.region_5.6_spmd, body=%wide.region_0.5_spmd.sunk | while | flops 38658048 | bytes 4834397 | solution.py:115
  38.8 1.4 %fusion.34 = (f32[8,256]{1,0:T(8,128)S(1)}, f32[8,256,256]{1,2,0:T(8,128)S(1)}) fusion(bf16[8,8,32,256]{3,2,1,0:T(8,128)(2,1)S(1)} %get-tuple-element.407, s32[]{:T(128)} %get-tuple-element.395, bf16[8,8,32,256]{3,2,1,0:T(8,128)(2,1)S(1)} %get-tuple-element.406, f32[8,256]{1,0:T(8,128)S(1)} %get-tuple-element.362, ...), kind=kOutput, calls=%fused_computation.64.clone.1 | convolution fusion | flops 37222400 | bytes 2393088 | tf_op jit(solution)/shard_map/while/body/eval_jaxpr/gdi,gdj->gij/dot_general | solution.py:95
  40.6 1.4 %fusion.34 = (f32[8,256]{1,0:T(8,128)S(1)}, f32[8,256,256]{1,2,0:T(8,128)S(1)}) fusion(bf16[8,8,32,256]{3,2,1,0:T(8,128)(2,1)S(1)} %get-tuple-element.407, s32[]{:T(128)} %get-tuple-element.395, bf16[8,8,32,256]{3,2,1,0:T(8,128)(2,1)S(1)} %get-tuple-element.406, f32[8,256]{1,0:T(8,128)S(1)} %get-tuple-element.362, ...), kind=kOutput, calls=%fused_computation.64.clone.1 | convolution fusion | flops 37222400 | bytes 2393088 | tf_op jit(solution)/shard_map/while/body/eval_jaxpr/gdi,gdj->gij/dot_general | solution.py:95
  42.5 1.4 %fusion.34 = (f32[8,256]{1,0:T(8,128)S(1)}, f32[8,256,256]{1,2,0:T(8,128)S(1)}) fusion(bf16[8,8,32,256]{3,2,1,0:T(8,128)(2,1)S(1)} %get-tuple-element.407, s32[]{:T(128)} %get-tuple-element.395, bf16[8,8,32,256]{3,2,1,0:T(8,128)(2,1)S(1)} %get-tuple-element.406, f32[8,256]{1,0:T(8,128)S(1)} %get-tuple-element.362, ...), kind=kOutput, calls=%fused_computation.64.clone.1 | convolution fusion | flops 37222400 | bytes 2393088 | tf_op jit(solution)/shard_map/while/body/eval_jaxpr/gdi,gdj->gij/dot_general | solution.py:95
  44.4 1.4 %fusion.34 = (f32[8,256]{1,0:T(8,128)S(1)}, f32[8,256,256]{1,2,0:T(8,128)S(1)}) fusion(bf16[8,8,32,256]{3,2,1,0:T(8,128)(2,1)S(1)} %get-tuple-element.407, s32[]{:T(128)} %get-tuple-element.395, bf16[8,8,32,256]{3,2,1,0:T(8,128)(2,1)S(1)} %get-tuple-element.406, f32[8,256]{1,0:T(8,128)S(1)} %get-tuple-element.362, ...), kind=kOutput, calls=%fused_computation.64.clone.1 | convolution fusion | flops 37222400 | bytes 2393088 | tf_op jit(solution)/shard_map/while/body/eval_jaxpr/gdi,gdj->gij/dot_general | solution.py:95
  46.2 1.4 %fusion.34 = (f32[8,256]{1,0:T(8,128)S(1)}, f32[8,256,256]{1,2,0:T(8,128)S(1)}) fusion(bf16[8,8,32,256]{3,2,1,0:T(8,128)(2,1)S(1)} %get-tuple-element.407, s32[]{:T(128)} %get-tuple-element.395, bf16[8,8,32,256]{3,2,1,0:T(8,128)(2,1)S(1)} %get-tuple-element.406, f32[8,256]{1,0:T(8,128)S(1)} %get-tuple-element.362, ...), kind=kOutput, calls=%fused_computation.64.clone.1 | convolution fusion | flops 37222400 | bytes 2393088 | tf_op jit(solution)/shard_map/while/body/eval_jaxpr/gdi,gdj->gij/dot_general | solution.py:95
  48.1 1.4 %fusion.34 = (f32[8,256]{1,0:T(8,128)S(1)}, f32[8,256,256]{1,2,0:T(8,128)S(1)}) fusion(bf16[8,8,32,256]{3,2,1,0:T(8,128)(2,1)S(1)} %get-tuple-element.407, s32[]{:T(128)} %get-tuple-element.395, bf16[8,8,32,256]{3,2,1,0:T(8,128)(2,1)S(1)} %get-tuple-element.406, f32[8,256]{1,0:T(8,128)S(1)} %get-tuple-element.362, ...), kind=kOutput, calls=%fused_computation.64.clone.1 | convolution fusion | flops 37222400 | bytes 2393088 | tf_op jit(solution)/shard_map/while/body/eval_jaxpr/gdi,gdj->gij/dot_general | solution.py:95
  50.0 1.4 %fusion.34 = (f32[8,256]{1,0:T(8,128)S(1)}, f32[8,256,256]{1,2,0:T(8,128)S(1)}) fusion(bf16[8,8,32,256]{3,2,1,0:T(8,128)(2,1)S(1)} %get-tuple-element.407, s32[]{:T(128)} %get-tuple-element.395, bf16[8,8,32,256]{3,2,1,0:T(8,128)(2,1)S(1)} %get-tuple-element.406, f32[8,256]{1,0:T(8,128)S(1)} %get-tuple-element.362, ...), kind=kOutput, calls=%fused_computation.64.clone.1 | convolution fusion | flops 37222400 | bytes 2393088 | tf_op jit(solution)/shard_map/while/body/eval_jaxpr/gdi,gdj->gij/dot_general | solution.py:95
  51.8 1.4 %fusion.34 = (f32[8,256]{1,0:T(8,128)S(1)}, f32[8,256,256]{1,2,0:T(8,128)S(1)}) fusion(bf16[8,8,32,256]{3,2,1,0:T(8,128)(2,1)S(1)} %get-tuple-element.407, s32[]{:T(128)} %get-tuple-element.395, bf16[8,8,32,256]{3,2,1,0:T(8,128)(2,1)S(1)} %get-tuple-element.406, f32[8,256]{1,0:T(8,128)S(1)} %get-tuple-element.362, ...), kind=kOutput, calls=%fused_computation.64.clone.1 | convolution fusion | flops 37222400 | bytes 2393088 | tf_op jit(solution)/shard_map/while/body/eval_jaxpr/gdi,gdj->gij/dot_general | solution.py:95
  53.8 0.7 multiply_subtract_fusion
  54.5 9.2 %all_gather.23 = f32[128,256]{1,0:T(8,128)S(1)} all-gather(f32[16,256]{1,0:T(8,128)S(1)} %multiply_subtract_fusion), channel_id=1, replica_groups=mesh['row'=4,'col'=8] {'col'}, dimensions={0}, use_global_device_ids=true | all-gather | bytes 147456 | tf_op jit(solution)/shard_map/all_gather | solution.py:129
  63.9 14.9 %while.47 = (s32[]{:T(128)}, f32[8,8,256]{2,1,0:T(8,128)S(1)}, f32[8,8,256]{2,1,0:T(8,128)S(1)}, f32[8,8,256]{2,1,0:T(8,128)S(1)}, bf16[8,8,32,256]{3,2,1,0:T(8,...) while((s32[]{:T(128)}, f32[8,8,256]{2,1,0:T(8,128)S(1)}, f32[8,8,256]{2,1,0:T(8,128)S(1)}, ...), condition=%wide.region_13.14_spmd, body=%wide.region_8.13_spmd.sunk | while | flops 38658048 | bytes 4834397 | solution.py:143
  64.0 1.4 %fusion.35 = (f32[8,256]{1,0:T(8,128)S(1)}, f32[8,256,256]{2,1,0:T(8,128)S(1)}) fusion(bf16[8,8,32,256]{3,2,1,0:T(8,128)(2,1)S(1)} %get-tuple-element.428, s32[]{:T(128)} %get-tuple-element.416, bf16[8,8,32,256]{3,2,1,0:T(8,128)(2,1)S(1)} %get-tuple-element.427, f32[8,256]{1,0:T(8,128)S(1)} %get-tuple-element.372, ...), kind=kOutput, calls=%fused_computation.65.clone.1 | convolution fusion | flops 37222400 | bytes 2393088 | tf_op jit(solution)/shard_map/while/body/eval_jaxpr/gdi,gdj->gij/dot_general | solution.py:95
  65.9 1.4 %fusion.35 = (f32[8,256]{1,0:T(8,128)S(1)}, f32[8,256,256]{2,1,0:T(8,128)S(1)}) fusion(bf16[8,8,32,256]{3,2,1,0:T(8,128)(2,1)S(1)} %get-tuple-element.428, s32[]{:T(128)} %get-tuple-element.416, bf16[8,8,32,256]{3,2,1,0:T(8,128)(2,1)S(1)} %get-tuple-element.427, f32[8,256]{1,0:T(8,128)S(1)} %get-tuple-element.372, ...), kind=kOutput, calls=%fused_computation.65.clone.1 | convolution fusion | flops 37222400 | bytes 2393088 | tf_op jit(solution)/shard_map/while/body/eval_jaxpr/gdi,gdj->gij/dot_general | solution.py:95
  67.8 1.4 %fusion.35 = (f32[8,256]{1,0:T(8,128)S(1)}, f32[8,256,256]{2,1,0:T(8,128)S(1)}) fusion(bf16[8,8,32,256]{3,2,1,0:T(8,128)(2,1)S(1)} %get-tuple-element.428, s32[]{:T(128)} %get-tuple-element.416, bf16[8,8,32,256]{3,2,1,0:T(8,128)(2,1)S(1)} %get-tuple-element.427, f32[8,256]{1,0:T(8,128)S(1)} %get-tuple-element.372, ...), kind=kOutput, calls=%fused_computation.65.clone.1 | convolution fusion | flops 37222400 | bytes 2393088 | tf_op jit(solution)/shard_map/while/body/eval_jaxpr/gdi,gdj->gij/dot_general | solution.py:95
  69.7 1.4 %fusion.35 = (f32[8,256]{1,0:T(8,128)S(1)}, f32[8,256,256]{2,1,0:T(8,128)S(1)}) fusion(bf16[8,8,32,256]{3,2,1,0:T(8,128)(2,1)S(1)} %get-tuple-element.428, s32[]{:T(128)} %get-tuple-element.416, bf16[8,8,32,256]{3,2,1,0:T(8,128)(2,1)S(1)} %get-tuple-element.427, f32[8,256]{1,0:T(8,128)S(1)} %get-tuple-element.372, ...), kind=kOutput, calls=%fused_computation.65.clone.1 | convolution fusion | flops 37222400 | bytes 2393088 | tf_op jit(solution)/shard_map/while/body/eval_jaxpr/gdi,gdj->gij/dot_general | solution.py:95
  71.5 1.4 %fusion.35 = (f32[8,256]{1,0:T(8,128)S(1)}, f32[8,256,256]{2,1,0:T(8,128)S(1)}) fusion(bf16[8,8,32,256]{3,2,1,0:T(8,128)(2,1)S(1)} %get-tuple-element.428, s32[]{:T(128)} %get-tuple-element.416, bf16[8,8,32,256]{3,2,1,0:T(8,128)(2,1)S(1)} %get-tuple-element.427, f32[8,256]{1,0:T(8,128)S(1)} %get-tuple-element.372, ...), kind=kOutput, calls=%fused_computation.65.clone.1 | convolution fusion | flops 37222400 | bytes 2393088 | tf_op jit(solution)/shard_map/while/body/eval_jaxpr/gdi,gdj->gij/dot_general | solution.py:95
  73.4 1.4 %fusion.35 = (f32[8,256]{1,0:T(8,128)S(1)}, f32[8,256,256]{2,1,0:T(8,128)S(1)}) fusion(bf16[8,8,32,256]{3,2,1,0:T(8,128)(2,1)S(1)} %get-tuple-element.428, s32[]{:T(128)} %get-tuple-element.416, bf16[8,8,32,256]{3,2,1,0:T(8,128)(2,1)S(1)} %get-tuple-element.427, f32[8,256]{1,0:T(8,128)S(1)} %get-tuple-element.372, ...), kind=kOutput, calls=%fused_computation.65.clone.1 | convolution fusion | flops 37222400 | bytes 2393088 | tf_op jit(solution)/shard_map/while/body/eval_jaxpr/gdi,gdj->gij/dot_general | solution.py:95
  75.3 1.4 %fusion.35 = (f32[8,256]{1,0:T(8,128)S(1)}, f32[8,256,256]{2,1,0:T(8,128)S(1)}) fusion(bf16[8,8,32,256]{3,2,1,0:T(8,128)(2,1)S(1)} %get-tuple-element.428, s32[]{:T(128)} %get-tuple-element.416, bf16[8,8,32,256]{3,2,1,0:T(8,128)(2,1)S(1)} %get-tuple-element.427, f32[8,256]{1,0:T(8,128)S(1)} %get-tuple-element.372, ...), kind=kOutput, calls=%fused_computation.65.clone.1 | convolution fusion | flops 37222400 | bytes 2393088 | tf_op jit(solution)/shard_map/while/body/eval_jaxpr/gdi,gdj->gij/dot_general | solution.py:95
  77.1 1.4 %fusion.35 = (f32[8,256]{1,0:T(8,128)S(1)}, f32[8,256,256]{2,1,0:T(8,128)S(1)}) fusion(bf16[8,8,32,256]{3,2,1,0:T(8,128)(2,1)S(1)} %get-tuple-element.428, s32[]{:T(128)} %get-tuple-element.416, bf16[8,8,32,256]{3,2,1,0:T(8,128)(2,1)S(1)} %get-tuple-element.427, f32[8,256]{1,0:T(8,128)S(1)} %get-tuple-element.372, ...), kind=kOutput, calls=%fused_computation.65.clone.1 | convolution fusion | flops 37222400 | bytes 2393088 | tf_op jit(solution)/shard_map/while/body/eval_jaxpr/gdi,gdj->gij/dot_general | solution.py:95
  78.9 3.7 %while.48 = (s32[]{:T(128)}, f32[2,32,256]{2,1,0:T(8,128)S(1)}, s32[64]{0:T(128)S(1)}, s32[2]{0:T(128)S(1)}, f32[8,8,256]{2,1,0:T(8,128)S(1)}, /*index=5*/s32[]{:T(128)}) while((s32[]{:T(128)}, f32[2,32,256]{2,1,0:T(8,128)S(1)}, s32[64]{0:T(128)S(1)}, s32[2]{0:T(128)S(1)}, f32[8,8,256]{2,1,0:T(8,128)S(1)}, /*index=5*/s32[]{:T(128)}) %tuple.90), condition=%wide.region_16.17_spmd, body=%wide.region_14.16_spmd.sunk | while | flops 1042466 | bytes 168537 | solution.py:58
  83.3 3.4 %all-to-all-start = ((f32[64,1,256]{2,1,0:T(1,128)}), f32[64,1,256]{2,1,0:T(1,128)S(1)}, u32[]{:S(2)}, u32[]{:S(2)}) async-start(f32[64,1,256]{2,1,0:T(1,128)} %broadcast_in_dim_reshape.4), calls=%async_computation | async-start | bytes 131072 | tf_op jit(solution)/shard_map/all_to_all | solution.py:149
  87.8 3.8 %all-to-all-done = f32[64,1,256]{2,1,0:T(1,128)S(1)} async-done(((f32[64,1,256]{2,1,0:T(1,128)}), f32[64,1,256]{2,1,0:T(1,128)S(1)}, u32[]{:S(2)}, u32[]{:S(2)}) %all-to-all-start) | async-done | bytes 65568 | tf_op jit(solution)/shard_map/all_to_all | solution.py:149
  91.6 3.3 %all-to-all-start.1 = ((f32[64,1,256]{2,1,0:T(1,128)}), f32[64,1,256]{2,1,0:T(1,128)S(1)}, u32[]{:S(2)}, u32[]{:S(2)}) async-start(f32[64,1,256]{2,1,0:T(1,128)} %copy.29), calls=%async_computation.1 | async-start | bytes 131072 | tf_op jit(solution)/shard_map/all_to_all | solution.py:150
  95.0 4.9 %all-to-all-done.1 = f32[64,1,256]{2,1,0:T(1,128)S(1)} async-done(((f32[64,1,256]{2,1,0:T(1,128)}), f32[64,1,256]{2,1,0:T(1,128)S(1)}, u32[]{:S(2)}, u32[]{:S(2)}) %all-to-all-start.1) | async-done | bytes 65568 | tf_op jit(solution)/shard_map/all_to_all | solution.py:150
  100.0 13.2 %all-gather.1 = f32[32,256]{1,0:T(8,128)S(1)} all-gather(f32[8,256]{1,0:T(8,128)S(1)} %fusion.16), channel_id=3, replica_groups=mesh['row'=4,'col'=8] {'row'}, dimensions={0}, use_global_device_ids=true | all-gather | bytes 40960 | tf_op jit(solution)/shard_map/all_gather | solution.py:19
  113.1 13.1 %all-gather = f32[32,256]{1,0:T(8,128)S(1)} all-gather(f32[8,256]{1,0:T(8,128)S(1)} %reduce_max.50), channel_id=2, replica_groups=mesh['row'=4,'col'=8] {'row'}, dimensions={0}, use_global_device_ids=true | all-gather | bytes 40960 | tf_op jit(solution)/shard_map/all_gather | solution.py:19
  (131 shorter events, 16.5 us)
Async XLA Ops:
  7.2 28.9 %all-gather.4.cloned.1.call-start = ((), (), s32[]{:S(2)}) async-start(), calls=%async_computation.2 | async-start | bytes 1179648 | tf_op jit(solution)/shard_map/all_gather | solution.py:76
  11.8 0.9 copy-start
  78.9 47.5 %copy-start.1 = (f32[8,256]{1,0:T(8,128)S(1)}, f32[8,256]{1,0:T(8,128)}, u32[]{:S(2)}) copy-start(f32[8,256]{1,0:T(8,128)} %param.17) | copy-start | bytes 24580
  83.3 8.3 %all-to-all-start = ((f32[64,1,256]{2,1,0:T(1,128)}), f32[64,1,256]{2,1,0:T(1,128)S(1)}, u32[]{:S(2)}, u32[]{:S(2)}) async-start(f32[64,1,256]{2,1,0:T(1,128)} %broadcast_in_dim_reshape.4), calls=%async_computation | async-start | bytes 131072 | tf_op jit(solution)/shard_map/all_to_all | solution.py:149
  91.6 8.3 %all-to-all-start.1 = ((f32[64,1,256]{2,1,0:T(1,128)}), f32[64,1,256]{2,1,0:T(1,128)S(1)}, u32[]{:S(2)}, u32[]{:S(2)}) async-start(f32[64,1,256]{2,1,0:T(1,128)} %copy.29), calls=%async_computation.1 | async-start | bytes 131072 | tf_op jit(solution)/shard_map/all_to_all | solution.py:150
Sparse Core Ops, SparseCore 0:
  9.9 26.1 all-gather.3
where the time goes:
time: 135 us
  blocking collectives  46.2 us (34%)
  matrix products  24.2 us (18%)
  waiting for transfers between devices  21.8 us (16%)
  between operations  14.3 us (11%)
  other arithmetic  10.1 us (7%)
  local copies, waits for them, and re-layouts  10.1 us (7%)
  starting transfers between devices  6.74 us (5%)
    all_gather x2, blocking collectives, joined(): pieces = jax.tree.map(lambda part: lax.all_gather(part, axis), value)  26.3 us
    dot_general x16, matrix products, distances(): jnp.einsum('gdi,gdj->gij', src_block, tgt_block, preferred_element_type=j...  22.4 us
    all_gather x1, waiting for transfers between devices, on_device(): all_points = lax.all_gather(tgt_points, 'col', axis=0, tiled=True)  12.4 us
    all_gather x1, blocking collectives, on_device(): all_potential = lax.all_gather(tgt_potential, 'col', axis=0, tiled=True)  10.7 us
    all_gather x1, blocking collectives, on_device(): src_new = lax.all_gather(own_new, 'col', axis=0, tiled=True)  9.15 us
    unnamed x8, local copies, waits for them, and re-layouts  6.32 us
    all_to_all x1, waiting for transfers between devices, on_device(): lax.all_to_all(target_total[:, None, :], 'col', split_axis=0, concat_axis...  4.89 us
    all_to_all x1, waiting for transfers between devices, on_device(): lax.all_to_all(target_top[:, None, :], 'col', split_axis=0, concat_axis=1...  3.85 us
  transfers between devices with their start and end apart: 3, of which 3 were waited for; matrix products, arithmetic and copies ran while one was open for 5% of the time, Pallas kernels for 0%

commit v1 on v0

v1 whole, which is shorter than its diff:
```python
import math

import jax
import jax.numpy as jnp
from jax import lax
from jax.experimental import pallas as pl
from jax.experimental.pallas import tpu as pltpu
from jax.sharding import PartitionSpec as P

epsilon = 0.1
very_low = -1e30
tiny_sum = 2.0**-100
log2_e = math.log2(math.e)
ln_2 = math.log(2.0)
depth = 128
tail_rows = 16
unroll = 4


def parts3(value):
    high = value.astype(jnp.bfloat16).astype(jnp.float32)
    rest = value - high
    middle = rest.astype(jnp.bfloat16).astype(jnp.float32)
    return high, middle, rest - middle


def lse2(left, right):
    top = jnp.maximum(left, right)
    low = jnp.minimum(left, right)
    return top + jnp.log2(1.0 + jnp.exp2(low - top))


def pad_rows(value, rows):
    return jnp.concatenate(
        [value, jnp.zeros((rows - value.shape[0],) + value.shape[1:], value.dtype)], axis=0
    )


def source_matrix(x_ref, tail_ref, s):
    x = x_ref[s]
    return pad_rows(jnp.concatenate([x, x, tail_ref[s]], axis=0), depth)


def tail_of(value, first):
    high, middle, low = parts3(value)
    row = lax.broadcasted_iota(jnp.int32, (tail_rows, value.shape[-1]), 0)
    ones_at, parts_at = (0, 3) if first else (3, 0)
    out = jnp.where((row >= ones_at) & (row < ones_at + 3), 1.0, 0.0)
    out = jnp.where(row == parts_at, high, out)
    out = jnp.where(row == parts_at + 1, middle, out)
    out = jnp.where(row == parts_at + 2, low, out)
    return out.astype(jnp.bfloat16)


def row_kernel(
    pattern_ref, own_ref, other_ref, own_pot_ref, other_pot_ref, src_ref,
    out_ref, y_ref, list_ref, count_ref,
    x_ref, tail_ref, z_ref, m_ref, s_count, sem,
):
    half, dim, cells = x_ref.shape
    own = own_ref.shape[0]
    pool = 2 * own
    fanout = pattern_ref.shape[1]
    scale = 2.0 * log2_e / (dim * epsilon)
    square_scale = log2_e / (dim * epsilon)
    col = lax.axis_index("col")
    core = lax.rem(col, 2)
    base = (col - core) * own
    flip = core * own
    copy = pltpu.make_async_copy(src_ref.at[pl.ds(core * half, half)], x_ref, sem)
    copy.start()

    def build_target(points_ref, pot_ref, offset):
        def body(t, _):
            y = points_ref[t].astype(jnp.float32)
            bias = pot_ref[pl.ds(t, 1), :] * (log2_e / epsilon) - square_scale * jnp.sum(
                y * y, axis=0, keepdims=True
            )
            scaled = y * scale
            high = scaled.astype(jnp.bfloat16)
            low = (scaled - high.astype(jnp.float32)).astype(jnp.bfloat16)
            stacked = pad_rows(
                jnp.concatenate([high, low, tail_of(bias, False)], axis=0), depth
            )
            y_ref[offset + t] = stacked.T
            return 0
        lax.fori_loop(0, own, body, 0)

    build_target(own_ref, own_pot_ref, 0)
    build_target(other_ref, other_pot_ref, own)
    top = jnp.maximum(jnp.max(own_pot_ref[...]), jnp.max(other_pot_ref[...])) * (
        log2_e / epsilon
    )

    def scan(s, count):
        s_total = jnp.int32(0)
        for k in range(fanout):
            t = pattern_ref[core * half + s, k] - base
            inside = jnp.where((t >= 0) & (t < pool), 1, 0)
            local = jnp.where(t >= own, t - own, t + own)
            local = jnp.where(core == 0, t, local)
            list_ref[count] = (s << 20) | (s << 8) | (local & 255)
            count = count + inside
            s_total = s_total + inside
        s_count[s] = s_total
        return count
    count = lax.fori_loop(0, half, scan, jnp.int32(0))
    for k in range(unroll):
        list_ref[count + k] = jnp.int32(half << 20)
    turns = (count + unroll - 1) // unroll
    count_ref[0] = turns

    copy.wait()

    def build_tail(s, _):
        x = x_ref[s].astype(jnp.float32)
        square = jnp.sum(x * x, axis=0, keepdims=True) * square_scale
        tail_ref[s] = tail_of(-square - top, True)
        z_ref[s] = jnp.zeros(z_ref.shape[1:], jnp.float32)
        return 0
    lax.fori_loop(0, half, build_tail, 0)

    def scores(entry):
        s = (entry >> 8) & 4095
        t = entry & 255
        return entry >> 20, jnp.dot(
            y_ref[t], source_matrix(x_ref, tail_ref, s), preferred_element_type=jnp.float32
        )

    def fast(turn, _):
        for k in range(unroll):
            row, a = scores(list_ref[turn * unroll + k])
            z_ref[row] += jnp.sum(jnp.exp2(a).reshape(cells // 8, 8, cells), axis=0)
        return 0
    lax.fori_loop(0, turns, fast, 0)

    def finish(s, bad):
        total = jnp.sum(z_ref[s], axis=0, keepdims=True)
        used = s_count[s] > 0
        out_ref[pl.ds(s, 1), :] = jnp.where(used, top + jnp.log2(total), very_low)
        return jnp.maximum(bad, jnp.where((total < tiny_sum) & used, 1.0, 0.0))
    bad = lax.fori_loop(0, half, finish, jnp.zeros((1, cells), jnp.float32))

    @pl.when(jnp.max(bad) > 0.0)
    def _():
        z_ref[...] = jnp.zeros_like(z_ref)
        m_ref[...] = jnp.full_like(m_ref, very_low)

        def slow(turn, _):
            row, a = scores(list_ref[turn])
            a = a.reshape(cells // 8, 8, cells)
            before = m_ref[row]
            after = jnp.maximum(before, jnp.max(a, axis=0))
            z_ref[row] = z_ref[row] * jnp.exp2(before - after) + jnp.sum(
                jnp.exp2(a - after[None]), axis=0
            )
            m_ref[row] = after
            return 0
        lax.fori_loop(0, count, slow, 0)

        def finish_slow(s, _):
            best = jnp.max(m_ref[s], axis=0, keepdims=True)
            total = jnp.sum(z_ref[s] * jnp.exp2(m_ref[s] - best), axis=0, keepdims=True)
            used = s_count[s] > 0
            out_ref[pl.ds(s, 1), :] = jnp.where(used, top + best + jnp.log2(total), very_low)
            return 0
        lax.fori_loop(0, half, finish_slow, 0)


def column_kernel(
    list_ref, count_ref, y_ref, l_ref, l2_ref, log_src_ref, src_ref,
    out_ref,
    x_ref, tail_ref, z_ref, m_ref, t_count, sem,
):
    half, dim, cells = x_ref.shape
    pool = y_ref.shape[0]
    square_scale = log2_e / (dim * epsilon)
    core = lax.rem(lax.axis_index("col"), 2)
    copy = pltpu.make_async_copy(src_ref.at[pl.ds(core * half, half)], x_ref, sem)
    copy.start()
    z_ref[...] = jnp.zeros_like(z_ref)
    turns = count_ref[0]
    for t in range(pool):
        t_count[t] = jnp.int32(0)
    copy.wait()

    def build_tail(s, _):
        x = x_ref[s].astype(jnp.float32)
        square = jnp.sum(x * x, axis=0, keepdims=True) * square_scale
        total = lse2(l_ref[pl.ds(s, 1), :], l2_ref[pl.ds(s, 1), :])
        mass = log_src_ref[pl.ds(core * half + s, 1), :] * log2_e
        tail_ref[s] = tail_of(mass - square - total, True)
        return 0
    lax.fori_loop(0, half, build_tail, 0)

    def scores(entry):
        s = (entry >> 8) & 4095
        t = entry & 255
        row = jnp.where((entry >> 20) == half, pool, t)
        return row, jnp.dot(
            y_ref[t], source_matrix(x_ref, tail_ref, s), preferred_element_type=jnp.float32
        )

    def fast(turn, _):
        for k in range(unroll):
            row, a = scores(list_ref[turn * unroll + k])
            e = jnp.exp2(a)
            z_ref[row] += e[:, :128] + e[:, 128:]
            t_count[row] = jnp.int32(1)
        return 0
    lax.fori_loop(0, turns, fast, 0)

    ones = jnp.ones((8, 128), jnp.float32)

    def finish(t, bad):
        total = lax.dot_general(
            ones, z_ref[t], (((1,), (1,)), ((), ())),
            precision=lax.Precision.HIGHEST, preferred_element_type=jnp.float32,
        )[0:1]
        used = t_count[t] > 0
        out_ref[pl.ds(t, 1), :] = jnp.where(used, jnp.log2(total), very_low)
        return jnp.maximum(bad, jnp.where((total < tiny_sum) & used, 1.0, 0.0))
    bad = lax.fori_loop(0, pool, finish, jnp.zeros((1, cells), jnp.float32))

    @pl.when(jnp.max(bad) > 0.0)
    def _():
        z_ref[...] = jnp.zeros_like(z_ref)
        m_ref[...] = jnp.full_like(m_ref, very_low)

        def slow(turn, _):
            row, a = scores(list_ref[turn])
            before = m_ref[row]
            after = jnp.maximum(before, jnp.maximum(a[:, :128], a[:, 128:]))
            z_ref[row] = (
                z_ref[row] * jnp.exp2(before - after)
                + jnp.exp2(a[:, :128] - after)
                + jnp.exp2(a[:, 128:] - after)
            )
            m_ref[row] = after
            return 0
        lax.fori_loop(0, turns * unroll, slow, 0)

        def finish_slow(t, _):
            best = jnp.max(m_ref[t], axis=1, keepdims=True)
            total = jnp.sum(z_ref[t] * jnp.exp2(m_ref[t] - best), axis=1, keepdims=True)
            column = jnp.broadcast_to(best + jnp.log2(total), (cells, 128))
            used = t_count[t] > 0
            out_ref[pl.ds(t, 1), :] = jnp.where(used, column.T[0:1], very_low)
            return 0
        lax.fori_loop(0, pool, finish_slow, 0)


def row_partials(pattern, own, other, own_pot, other_pot, src_points):
    sources, dim, cells = src_points.shape
    half = sources // 2
    pool = 2 * own.shape[0]
    most = half * pattern.shape[1] + unroll
    smem = pl.BlockSpec(memory_space=pltpu.SMEM)
    vmem = pl.BlockSpec(memory_space=pltpu.VMEM)
    return pl.pallas_call(
        row_kernel,
        name="row_half_step",
        out_shape=(
            jax.ShapeDtypeStruct((half, cells), jnp.float32),
            jax.ShapeDtypeStruct((pool, cells, depth), jnp.bfloat16),
            jax.ShapeDtypeStruct((most,), jnp.int32),
            jax.ShapeDtypeStruct((1,), jnp.int32),
        ),
        in_specs=[smem, vmem, vmem, vmem, vmem, pl.BlockSpec(memory_space=pl.ANY)],
        out_specs=(vmem, vmem, smem, smem),
        scratch_shapes=[
            pltpu.VMEM((half, dim, cells), jnp.bfloat16),
            pltpu.VMEM((half, tail_rows, cells), jnp.bfloat16),
            pltpu.VMEM((half + 1, 8, cells), jnp.float32),
            pltpu.VMEM((half + 1, 8, cells), jnp.float32),
            pltpu.SMEM((half,), jnp.int32),
            pltpu.SemaphoreType.DMA,
        ],
    )(pattern, own, other, own_pot, other_pot, src_points)


def column_partials(pair_list, turns, targets, left, right, log_src, src_points):
    sources, dim, cells = src_points.shape
    half = sources // 2
    pool = targets.shape[0]
    smem = pl.BlockSpec(memory_space=pltpu.SMEM)
    vmem = pl.BlockSpec(memory_space=pltpu.VMEM)
    return pl.pallas_call(
        column_kernel,
        name="column_half_step",
        out_shape=jax.ShapeDtypeStruct((pool, cells), jnp.float32),
        in_specs=[smem, smem, vmem, vmem, vmem, vmem, pl.BlockSpec(memory_space=pl.ANY)],
        out_specs=vmem,
        scratch_shapes=[
            pltpu.VMEM((half, dim, cells), jnp.bfloat16),
            pltpu.VMEM((half, tail_rows, cells), jnp.bfloat16),
            pltpu.VMEM((pool + 1, cells, 128), jnp.float32),
            pltpu.VMEM((pool + 1, cells, 128), jnp.float32),
            pltpu.SMEM((pool + 1,), jnp.int32),
            pltpu.SemaphoreType.DMA,
        ],
    )(pair_list, turns, targets, left, right, log_src, src_points)


def solution(mesh):
    rows, cols = mesh.shape["row"], mesh.shape["col"]

    def swap(value, axis, step):
        size = mesh.shape[axis]
        return lax.ppermute(value, axis, [(i, i ^ step) for i in range(size)])

    def on_device(src_points, tgt_points, log_src, log_tgt, tgt_potential, pattern):
        half = src_points.shape[0] // 2
        own = tgt_points.shape[0]
        core = lax.rem(lax.axis_index("col"), 2)
        other_points = swap(tgt_points, "col", 1)
        other_potential = swap(tgt_potential, "col", 1)
        left, targets, pair_list, turns = row_partials(
            pattern, tgt_points, other_points, tgt_potential, other_potential, src_points
        )
        step = 2
        right = jnp.full_like(left, very_low)
        while step < cols:
            left = lse2(left, right) if step > 2 else left
            right = swap(left, "col", step)
            step *= 2
        own_log = lax.dynamic_slice_in_dim(log_src, core * half, half, 0)
        own_new = epsilon * own_log - (epsilon * ln_2) * lse2(left, right)
        other_new = swap(own_new, "col", 1)
        src_new = jnp.concatenate(
            [jnp.where(core == 0, own_new, other_new), jnp.where(core == 0, other_new, own_new)]
        )
        sums = column_partials(pair_list, turns, targets, left, right, log_src, src_points)
        total = lse2(sums[:own], swap(sums[own:], "col", 1))
        step = 1
        while step < rows:
            total = lse2(total, swap(total, "row", step))
            step *= 2
        tgt_new = epsilon * log_tgt - (epsilon * ln_2) * total + tgt_potential
        return (src_new, tgt_new)

    placed = (
        P("row", None, None),
        P("col", None, None),
        P("row", None),
        P("col", None),
        P("col", None),
        P("row", None),
    )
    return jax.shard_map(
        on_device,
        mesh=mesh,
        in_specs=placed,
        out_specs=(P("row", None), P("col", None)),
        check_vma=False,
    )
```

time: 135 us -> 112 us (0.83)
  the two profiles are of different devices: /device:TPU:0 before, /device:TPU:12 now
where the time goes in v1:
time: 112 us
  Pallas kernels  66.8 us (60%)
  starting transfers between devices  20.3 us (18%)
  waiting for transfers between devices  16.4 us (15%)
  local copies, waits for them, and re-layouts  3.99 us (4%)
  other arithmetic  3.82 us (3%)
    pallas_call x1, Pallas kernels, column_partials(): pl.pallas_call(column_kernel, name='column_half_step', out_shape=jax.Shap...  34 us
    pallas_call x1, Pallas kernels, row_partials(): pl.pallas_call(row_kernel, name='row_half_step', out_shape=(jax.ShapeDtyp...  32.8 us
    ppermute x8, starting transfers between devices, swap(): return lax.ppermute(value, axis, [(i, i ^ step) for i in range(size)])  20.3 us
    ppermute x8, waiting for transfers between devices, swap(): return lax.ppermute(value, axis, [(i, i ^ step) for i in range(size)])  16.4 us
    unnamed x15, local copies, waits for them, and re-layouts  3.3 us
  transfers between devices with their start and end apart: 8, of which 5 were waited for; matrix products, arithmetic and copies ran while one was open for 3% of the time, Pallas kernels for 0%

profile of v1, /device:TPU:12, one launch (start us, length us, event | category | flops | bytes accessed | tf_op | source)
XLA Modules:
  0.0 112.1 jit_solution(17446168500122646300)
XLA Ops:
  0.6 0.1 collective-permute-start
  0.7 0.5 collective-permute-start.1
  1.2 1.4 %copy.8.pattern_ref = s32[128,4]{1,0:T(8,128)} copy(s32[128,4]{0,1:T(4,128)} %param.11) | data formatting | bytes 4096 | tf_op args[5]
  2.6 0.0 collective-permute-done.1.other_pot_ref
  2.6 0.0 collective-permute-done.other_ref
  2.6 0.6 copy-done.5
  3.2 0.7 copy-done.3
  3.9 32.8 %row_half_step.1 = (f32[64,256]{1,0:T(8,128)}, bf16[16,256,128]{2,1,0:T(8,128)(2,1)}, s32[260]{0:T(512)}, s32[1]{0:T(128)}) custom-call(s32[128,4]{1,0:T(8,128)} %copy.8.pattern_ref, bf16[8,32,256]{2,1,0:T(8,128)(2,1)} %own_ref.1, bf16[8,32,256]{2,1,0:T(8,128)(2,1)} %copy-done.3, f32[8,256]{1,0:T(8,128)} %own_pot_ref.1, f32[8,256]{1,0:T(8,128)} %copy-done.5, ...), custom_call_target="tpu_custom_call" | custom-call | tf_op jit(solution)/shard_map/row_half_step/pallas_call | solution.py:260
  36.7 0.0 copy-start.1
  36.7 0.0 copy-start.4
  36.7 0.0 copy-start.6
  36.7 0.1 collective-permute-start.2
  36.8 4.5 %collective-permute-done.2 = f32[64,256]{1,0:T(8,128)S(1)} collective-permute-done((f32[64,256]{1,0:T(8,128)}, f32[64,256]{1,0:T(8,128)S(1)}, u32[]{:S(2)}, u32[]{:S(2)}) %collective-permute-start.2) | collective-permute-done | bytes 65568 | tf_op jit(solution)/shard_map/ppermute | solution.py:310
  41.3 0.9 multiply_add_fusion.l_ref
  42.1 0.0 copy-start
  42.1 0.4 collective-permute-start.3
  42.5 3.9 %collective-permute-done.3.l2_ref = f32[64,256]{1,0:T(8,128)S(1)} collective-permute-done((f32[64,256]{1,0:T(8,128)S(1)}, f32[64,256]{1,0:T(8,128)S(1)}, u32[]{:S(2)}, u32[]{:S(2)}) %collective-permute-start.3) | collective-permute-done | bytes 65568 | tf_op jit(solution)/shard_map/ppermute | solution.py:310
  46.5 0.6 copy-done.2
  47.1 34.0 %column_half_step.1 = f32[16,256]{1,0:T(8,128)} custom-call(s32[260]{0:T(512)} %get-tuple-element.7.list_ref, s32[1]{0:T(128)} %get-tuple-element.8.count_ref, bf16[16,256,128]{2,1,0:T(8,128)(2,1)} %get-tuple-element.9.y_ref, f32[64,256]{1,0:T(8,128)} %copy-done, f32[64,256]{1,0:T(8,128)} %copy-done.2, f32[128,256]{1,0:T(8,128)} %log_src_ref.1, ...), custom_call_target="tpu_custom_call" | custom-call | tf_op jit(solution)/shard_map/column_half_step/pallas_call | solution.py:288
  81.1 0.7 slice.9
  81.8 19.1 %collective-permute-start.5 = (f32[8,256]{1,0:T(8,128)S(1)}, f32[8,256]{1,0:T(8,128)S(1)}, u32[]{:S(2)}, u32[]{:S(2)}) collective-permute-start(f32[8,256]{1,0:T(8,128)S(1)} %slice.9), channel_id=1, source_target_pairs={{0,1},{1,0},{2,3},{3,2},{4,5},{5,4},{6,7},{7,6},{8,9},{9,8},{10,11... | collective-permute-start | bytes 24584 | tf_op jit(solution)/shard_map/ppermute | solution.py:310
  100.9 0.8 collective-permute-done.5
  101.7 0.7 multiply_add_fusion.2
  102.4 0.1 collective-permute-start.6
  102.5 3.6 %collective-permute-done.6 = f32[8,256]{1,0:T(8,128)S(1)} collective-permute-done((f32[8,256]{1,0:T(8,128)S(1)}, f32[8,256]{1,0:T(8,128)S(1)}, u32[]{:S(2)}, u32[]{:S(2)}) %collective-permute-start.6) | collective-permute-done | bytes 8224 | tf_op jit(solution)/shard_map/ppermute | solution.py:310
  106.2 0.1 collective-permute-start.7
  106.3 0.9 multiply_subtract_fusion
  107.2 0.1 collective-permute-start.4
  107.3 3.5 %collective-permute-done.7 = f32[8,256]{1,0:T(8,128)S(1)} collective-permute-done((f32[8,256]{1,0:T(8,128)S(1)}, f32[8,256]{1,0:T(8,128)S(1)}, u32[]{:S(2)}, u32[]{:S(2)}) %collective-permute-start.7) | collective-permute-done | bytes 8224 | tf_op jit(solution)/shard_map/ppermute | solution.py:310
  110.8 0.6 subtract_add_fusion
  111.4 0.0 collective-permute-done.4
  111.4 0.7 pad_maximum_fusion
  (9 shorter events, 0.0 us)
Async XLA Ops:
  0.6 2.0 %collective-permute-start = (bf16[8,32,256]{2,1,0:T(8,128)(2,1)}, bf16[8,32,256]{2,1,0:T(8,128)(2,1)S(1)}, u32[]{:S(2)}, u32[]{:S(2)}) collective-permute-start(bf16[8,32,256]{2,1,0:T(8,128)(2,1)} %own_ref.1), channel_id=1, source_target_pairs={{0,1},{1,0},{2,3},{3,2},{4,5},{5,4},{6,7},{7,6},{8,9},{9,8},{10,11... | collective-permute-start | bytes 393224 | tf_op jit(solution)/shard_map/ppermute | solution.py:310
  0.7 1.9 %collective-permute-start.1 = (f32[8,256]{1,0:T(8,128)}, f32[8,256]{1,0:T(8,128)S(1)}, u32[]{:S(2)}, u32[]{:S(2)}) collective-permute-start(f32[8,256]{1,0:T(8,128)} %own_pot_ref.1), channel_id=1, source_target_pairs={{0,1},{1,0},{2,3},{3,2},{4,5},{5,4},{6,7},{7,6},{8,9},{9,8},{10,11... | collective-permute-start | bytes 24584 | tf_op jit(solution)/shard_map/ppermute | solution.py:310
  2.6 0.6 copy-start.5
  3.2 0.7 copy-start.3
  36.7 69.6 %copy-start.1 = (f32[128,256]{1,0:T(8,128)S(1)}, f32[128,256]{1,0:T(8,128)}, u32[]{:S(2)}) copy-start(f32[128,256]{1,0:T(8,128)} %log_src_ref.1) | copy-start | bytes 393220
  36.7 74.1 %copy-start.4 = (f32[8,256]{1,0:T(8,128)S(1)}, f32[8,256]{1,0:T(8,128)}, u32[]{:S(2)}) copy-start(f32[8,256]{1,0:T(8,128)} %own_pot_ref.1) | copy-start | bytes 24580
  36.7 74.1 %copy-start.6 = (f32[8,256]{1,0:T(8,128)S(1)}, f32[8,256]{1,0:T(8,128)}, u32[]{:S(2)}) copy-start(f32[8,256]{1,0:T(8,128)} %param.9) | copy-start | bytes 24580
  36.7 4.5 %collective-permute-start.2 = (f32[64,256]{1,0:T(8,128)}, f32[64,256]{1,0:T(8,128)S(1)}, u32[]{:S(2)}, u32[]{:S(2)}) collective-permute-start(f32[64,256]{1,0:T(8,128)} %get-tuple-element.6), channel_id=1, source_target_pairs={{0,2},{1,3},{2,0},{3,1},{4,6},{5,7},{6,4},{7,5},{8,10},{9,11},{10,... | collective-permute-start | bytes 196616 | tf_op jit(solution)/shard_map/ppermute | solution.py:310
  42.1 4.3 %copy-start = (f32[64,256]{1,0:T(8,128)}, f32[64,256]{1,0:T(8,128)S(1)}, u32[]{:S(2)}) copy-start(f32[64,256]{1,0:T(8,128)S(1)} %multiply_add_fusion.l_ref) | copy-start | bytes 196612
  42.1 4.3 %collective-permute-start.3 = (f32[64,256]{1,0:T(8,128)S(1)}, f32[64,256]{1,0:T(8,128)S(1)}, u32[]{:S(2)}, u32[]{:S(2)}) collective-permute-start(f32[64,256]{1,0:T(8,128)S(1)} %multiply_add_fusion.l_ref), channel_id=1, source_target_pairs={{0,4},{1,5},{2,6},{3,7},{4,0},{5,1},{6,2},{7,3},{8,12},{9,13},{10,... | collective-permute-start | bytes 196616 | tf_op jit(solution)/shard_map/ppermute | solution.py:310
  46.5 0.6 copy-start.2
  81.8 19.9 %collective-permute-start.5 = (f32[8,256]{1,0:T(8,128)S(1)}, f32[8,256]{1,0:T(8,128)S(1)}, u32[]{:S(2)}, u32[]{:S(2)}) collective-permute-start(f32[8,256]{1,0:T(8,128)S(1)} %slice.9), channel_id=1, source_target_pairs={{0,1},{1,0},{2,3},{3,2},{4,5},{5,4},{6,7},{7,6},{8,9},{9,8},{10,11... | collective-permute-start | bytes 24584 | tf_op jit(solution)/shard_map/ppermute | solution.py:310
  102.4 3.7 %collective-permute-start.6 = (f32[8,256]{1,0:T(8,128)S(1)}, f32[8,256]{1,0:T(8,128)S(1)}, u32[]{:S(2)}, u32[]{:S(2)}) collective-permute-start(f32[8,256]{1,0:T(8,128)S(1)} %multiply_add_fusion.2), channel_id=1, source_target_pairs={{0,8},{8,0},{16,24},{24,16},{1,9},{9,1},{17,25},{25,17},{2,10},{10... | collective-permute-start | bytes 24584 | tf_op jit(solution)/shard_map/ppermute | solution.py:310
  106.2 4.6 %collective-permute-start.7 = (f32[8,256]{1,0:T(8,128)S(1)}, f32[8,256]{1,0:T(8,128)S(1)}, u32[]{:S(2)}, u32[]{:S(2)}) collective-permute-start(f32[8,256]{1,0:T(8,128)S(1)} %multiply_add_fusion.1), channel_id=1, source_target_pairs={{0,16},{8,24},{16,0},{24,8},{1,17},{9,25},{17,1},{25,9},{2,18},{10... | collective-permute-start | bytes 24584 | tf_op jit(solution)/shard_map/ppermute | solution.py:310
  107.2 4.2 %collective-permute-start.4 = (f32[64,256]{1,0:T(8,128)S(1)}, f32[64,256]{1,0:T(8,128)S(1)}, u32[]{:S(2)}, u32[]{:S(2)}) collective-permute-start(f32[64,256]{1,0:T(8,128)S(1)} %multiply_subtract_fusion), channel_id=1, source_target_pairs={{0,1},{1,0},{2,3},{3,2},{4,5},{5,4},{6,7},{7,6},{8,9},{9,8},{10,11... | collective-permute-start | bytes 196616 | tf_op jit(solution)/shard_map/ppermute | solution.py:310
